TPU v7x, 32 devices: a whole 2x2x4 slice. The times are simulated.
32 devices in a mesh: page: 8 (over z, x), seq: 4 (over y, core).
Axes of the slice: x: 2, y: 2, z: 4, core: 2. Of those that a mesh axis runs over, the one named last changes fastest.
Arguments:
- tokens: bfloat16 [16, 512, 1024], P('page', 'seq'), may hold values from -6 to 6
- cells: int32 [16, 512], P('page', 'seq'), may hold values from 0 to 511, as said below
- lengths: int32 [16], P('page'), may hold values from 64 to 512, as said below
- cotangent: bfloat16 [16, 512, 1024], P('page', 'seq'), may hold values from -6 to 6
- w_qkv: float32 [1024, 3072], P(('page', 'seq')), may hold values from -0.1875 to 0.1875
- w_out: float32 [1024, 1024], P(('page', 'seq')), may hold values from -0.75 to 0.75
- w_up: float32 [1024, 4096], P(('page', 'seq')), may hold values from -0.1875 to 0.1875
- w_down: float32 [4096, 1024], P(('page', 'seq')), may hold values from -0.09375 to 0.09375
- biases: float32 [10, 1024], P(None, ('page', 'seq')), may hold values from -3 to 3
- gains: float32 [2, 1024], P(None, ('page', 'seq')), may hold values from 0.5 to 1.5
- cell_bias: float32 [16], replicated, may hold values from 0.5 to 2
Outputs:
- output: bfloat16 [16, 512, 1024], P('page', 'seq')
- grad_tokens: float32 [16, 512, 1024], P('page', 'seq')
- grad_qkv: float32 [1024, 3072], P(('page', 'seq'))
- grad_out: float32 [1024, 1024], P(('page', 'seq'))
- grad_up: float32 [1024, 4096], P(('page', 'seq'))
- grad_down: float32 [4096, 1024], P(('page', 'seq'))
- grad_biases: float32 [10, 1024], P(None, ('page', 'seq'))
- grad_gains: float32 [2, 1024], P(None, ('page', 'seq'))
- grad_cell: float32 [16], replicated
Inputs may be any that keep to these rules, and one draw needn't show every extreme that they name: `lengths`: every page has at least 64 valid tokens, and some page is full. `cells`: within a page cell numbers never fall, rise by at most one from token to token, and the first token is in cell 0; some page has every token in a cell of its own.
All inputs are finite; a program needn't handle non-finite values.
Results may differ from a plain program's by a relative error of at most 0.014.
The roundings to bfloat16 on the way count: a program that leaves them out, or rounds other values in their place, can miss the bound.
Values may be sent and summed in bfloat16 or wider, within the bound.
No kernel may reach another device: no remote copies, remote signals or barrier semaphores. Data moves between devices by JAX's collectives and lax.ppermute only.
A program may use at most 256 MiB of HBM per device.

v0:
```python
import jax
import jax.numpy as jnp
from jax import lax
from jax.sharding import PartitionSpec as P

LOW = jnp.bfloat16
WIDE = jnp.float32


def layer_norm(values, gain, shift):
    center = values - jnp.mean(values, axis=-1, keepdims=True)
    spread = jnp.mean(center * center, axis=-1, keepdims=True)
    return center * lax.rsqrt(spread + 1e-05) * gain + shift


def gelu_exact(values):
    return 0.5 * values * (1.0 + jax.scipy.special.erf(values * 0.7071067811865476))


def swap(values, axis, count, mask):
    return lax.ppermute(values, axis, [(i, i ^ mask) for i in range(count)])


def bits_of(count):
    return [1 << k for k in range(count.bit_length() - 1)]


def gather_bits(values, axis, count, dim, order):
    index = lax.axis_index(axis)
    done = []
    for mask in order:
        other = swap(values, axis, count, mask)
        place = dim + sum((1 for m in done if m > mask))
        first = index // mask % 2 == 0
        values = jnp.stack(
            [jnp.where(first, values, other), jnp.where(first, other, values)], axis=place
        )
        done.append(mask)
    shape = values.shape
    rest = shape[dim + len(order) :]
    return values.reshape(shape[:dim] + (count,) + rest)


def scatter_bits(values, axis, count, dim, order):
    index = lax.axis_index(axis)
    left = sorted(order, reverse=True)
    shape = values.shape
    values = values.reshape(shape[:dim] + (2,) * len(left) + shape[dim + 1 :])
    for mask in order:
        at = dim + left.index(mask)
        bit = index // mask % 2
        keep = lax.dynamic_index_in_dim(values, bit, at, keepdims=False)
        send = lax.dynamic_index_in_dim(values, 1 - bit, at, keepdims=False)
        values = keep.astype(WIDE) + swap(send.astype(LOW), axis, count, mask).astype(WIDE)
        left.remove(mask)
    return values


def local(
    counts, tokens, cells, lengths, cotangent, w_qkv, w_out, w_up, w_down, biases, gains, cell_bias
):
    pages, seqs = counts
    page_count, row_count, width = tokens.shape
    slots = row_count * seqs
    heads = cell_bias.shape[0]
    depth = width // heads
    heads_here = heads // seqs
    span = heads_here * depth
    flat = page_count * row_count
    rows = w_qkv.shape[0]
    ff_rows = w_down.shape[0]
    ff_here = ff_rows * pages
    seq_index = lax.axis_index("seq")
    high_page = bits_of(pages)[::-1]
    low_page = bits_of(pages)
    high_seq = bits_of(seqs)[::-1]
    low_seq = bits_of(seqs)

    def gather_seq(values, dim):
        return gather_bits(values, "seq", seqs, dim, high_seq)

    def scatter_seq(values, dim):
        return scatter_bits(values, "seq", seqs, dim, low_seq)

    def turn(values):
        return lax.all_to_all(values, "seq", 0, 0)

    part_qkv = w_qkv.astype(LOW).reshape(rows, 3, seqs, span).transpose(2, 0, 1, 3)
    part_qkv = turn(part_qkv.reshape(seqs, rows, 3 * span)).reshape(seqs * rows, 3 * span)
    w_proj = gather_bits(part_qkv, "page", pages, 0, high_page).reshape(width, 3 * span)
    small = jnp.concatenate([biases, gains], axis=0).astype(LOW)
    small_rows = small.shape[0]
    small_pad = -(-small.size // width)
    small_pad = -(-small_pad // 8) * 8
    small_flat = jnp.pad(small.reshape(-1), (0, small_pad * width - small.size)).reshape(
        small_pad, width
    )
    both = lax.all_gather(
        jnp.concatenate([w_out.astype(LOW), small_flat], axis=0),
        ("page", "seq"),
        axis=0,
        tiled=False,
    )
    w_mix = both[:, :rows].reshape(width, width)
    lanes = small.shape[1]
    vectors = both[:, rows:].reshape(pages * seqs, small_pad * width)[:, : small.size]
    vectors = vectors.reshape(pages * seqs, small_rows, lanes).transpose(1, 0, 2)
    vectors = vectors.reshape(small_rows, width).astype(WIDE)
    scales = vectors[small_rows - 2 :]
    part_up = w_up.astype(LOW).reshape(rows, pages, seqs, ff_rows).transpose(2, 0, 1, 3)
    part_up = turn(part_up.reshape(seqs, rows, ff_here)).reshape(seqs * rows, ff_here)
    w_expand = gather_bits(part_up, "page", pages, 0, high_page).reshape(width, ff_here)
    w_reduce = gather_bits(w_down.astype(LOW), "page", pages, 0, high_page).reshape(ff_here, width)
    hidden_bias = vectors[6:10].reshape(pages, seqs, ff_rows)
    hidden_bias = lax.dynamic_index_in_dim(hidden_bias, seq_index, 1, keepdims=False).reshape(
        ff_here
    )
    everything = gather_seq(tokens, 1).reshape(page_count * slots, width)
    cells_all = lax.all_gather(cells, "seq", axis=1, tiled=True)
    bias_q = lax.dynamic_slice_in_dim(vectors[0], seq_index * span, span)
    bias_v = lax.dynamic_slice_in_dim(vectors[1], seq_index * span, span)
    bias_qkv = jnp.concatenate([bias_q, jnp.zeros_like(bias_q), bias_v])
    projected = (jnp.dot(everything, w_proj, preferred_element_type=WIDE) + bias_qkv).astype(LOW)
    projected = projected.reshape(page_count, slots, 3, heads_here, depth)
    query, keys, values = (projected[:, :, 0], projected[:, :, 1], projected[:, :, 2])
    own_bias = lax.dynamic_slice_in_dim(cell_bias, seq_index * heads_here, heads_here)
    same_cell = (cells_all[:, :, None] == cells_all[:, None, :]).astype(WIDE)
    key_valid = lax.broadcasted_iota(jnp.int32, (page_count, slots), 1) < lengths[:, None]

    def scores_of():
        raw = jnp.einsum("pqhe,pkhe->phqk", query, keys, preferred_element_type=WIDE) * 0.125
        scores = raw + own_bias[None, :, None, None] * same_cell[:, None]
        return jnp.where(key_valid[:, None, None, :], scores, -1e30)

    scores = scores_of()
    peak = jnp.max(scores, axis=-1, keepdims=True)
    exponent = jnp.exp(scores - peak)
    totals = jnp.sum(exponent, axis=-1, keepdims=True)
    log_total = peak + jnp.log(totals)
    weights_low = (exponent / totals).astype(LOW)
    context_here = jnp.einsum("phqk,pkhe->pqhe", weights_low, values, preferred_element_type=WIDE)
    context_here = context_here.astype(LOW).reshape(page_count, seqs, row_count, span)
    context = turn(context_here.transpose(1, 0, 2, 3)).transpose(1, 2, 0, 3).reshape(flat, width)
    inputs_wide = tokens.reshape(flat, width).astype(WIDE)
    attended = jnp.dot(context, w_mix, preferred_element_type=WIDE) + vectors[2]
    normed, norm_first = jax.vjp(layer_norm, inputs_wide + attended, scales[0], vectors[4])
    normed_all = gather_seq(normed.astype(LOW), 0).reshape(seqs * flat, width)
    expanded = jnp.dot(normed_all, w_expand, preferred_element_type=WIDE) + hidden_bias
    activated, gelu_back = jax.vjp(gelu_exact, expanded)
    activated_low = activated.astype(LOW)
    reduced = jnp.dot(activated_low, w_reduce, preferred_element_type=WIDE)
    reduced = scatter_seq(reduced.reshape(seqs, flat, width), 0) + vectors[3]
    output_wide, norm_second = jax.vjp(layer_norm, normed + reduced, scales[1], vectors[5])
    output = output_wide.astype(LOW).reshape(page_count, row_count, width)
    grad_second, grad_gain_two, grad_shift_two = norm_second(
        cotangent.reshape(flat, width).astype(WIDE)
    )
    second_all = gather_seq(grad_second.astype(LOW), 0).reshape(seqs * flat, width)
    grad_activated = jnp.einsum("td,fd->tf", second_all, w_reduce, preferred_element_type=WIDE)
    grad_expanded = gelu_back(grad_activated)[0]
    expanded_low = grad_expanded.astype(LOW)
    grad_normed = jnp.einsum("tf,df->td", expanded_low, w_expand, preferred_element_type=WIDE)
    grad_normed = grad_second + scatter_seq(grad_normed.reshape(seqs, flat, width), 0)
    grad_reduce = jnp.einsum("tf,td->fd", activated_low, second_all, preferred_element_type=WIDE)
    grad_reduce = scatter_bits(
        grad_reduce.reshape(pages, ff_rows, width), "page", pages, 0, low_page
    )
    grad_expand = jnp.einsum("td,tf->df", normed_all, expanded_low, preferred_element_type=WIDE)
    grad_expand = scatter_bits(
        grad_expand.reshape(pages, seqs * rows, ff_here), "page", pages, 0, low_page
    )
    grad_expand = turn(grad_expand.astype(LOW).reshape(seqs, rows, ff_here))
    grad_expand = grad_expand.reshape(seqs, rows, pages, ff_rows).transpose(1, 2, 0, 3)
    grad_expand = grad_expand.reshape(rows, seqs * ff_here).astype(WIDE)
    grad_first, grad_gain_one, grad_shift_one = norm_first(grad_normed)
    first_low = grad_first.astype(LOW)
    grad_context = jnp.einsum("td,cd->tc", first_low, w_mix, preferred_element_type=WIDE).astype(
        LOW
    )
    grad_context = grad_context.reshape(page_count, row_count, seqs, span).transpose(2, 0, 1, 3)
    grad_context = (
        turn(grad_context).transpose(1, 0, 2, 3).reshape(page_count, slots, heads_here, depth)
    )
    grad_mix = jnp.einsum("tc,td->cd", context, first_low, preferred_element_type=WIDE)
    grad_mix = scatter_bits(grad_mix.reshape(pages, seqs, rows, width), "seq", seqs, 1, low_seq)
    grad_mix = scatter_bits(grad_mix, "page", pages, 0, low_page)
    weights_wide = jnp.exp(scores_of() - log_total)
    weights_low = weights_wide.astype(LOW)
    grad_weights = jnp.einsum("pqhe,pkhe->phqk", grad_context, values, preferred_element_type=WIDE)
    inner = jnp.sum(weights_wide * grad_weights, axis=-1, keepdims=True)
    grad_scores = weights_wide * (grad_weights - inner)
    grad_cell = jnp.sum(grad_scores * same_cell[:, None], axis=(0, 2, 3))
    scores_low = grad_scores.astype(LOW)
    grad_values = jnp.einsum(
        "phqk,pqhe->pkhe", weights_low, grad_context, preferred_element_type=WIDE
    )
    grad_query = (
        jnp.einsum("phqk,pkhe->pqhe", scores_low, keys, preferred_element_type=WIDE) * 0.125
    )
    grad_keys = (
        jnp.einsum("phqk,pqhe->pkhe", scores_low, query, preferred_element_type=WIDE) * 0.125
    )
    grad_proj_low = jnp.stack([grad_query, grad_keys, grad_values], axis=2).astype(LOW)
    grad_proj_low = grad_proj_low.reshape(page_count * slots, 3 * span)
    grad_proj = jnp.einsum("td,tc->dc", everything, grad_proj_low, preferred_element_type=WIDE)
    grad_proj = scatter_bits(
        grad_proj.reshape(pages, seqs * rows, 3 * span), "page", pages, 0, low_page
    )
    grad_proj = turn(grad_proj.astype(LOW).reshape(seqs, rows, 3 * span))
    grad_proj = (
        grad_proj.reshape(seqs, rows, 3, span).transpose(1, 2, 0, 3).reshape(rows, 3 * width)
    )
    grad_proj = grad_proj.astype(WIDE)
    grad_inputs = jnp.einsum("tc,dc->td", grad_proj_low, w_proj, preferred_element_type=WIDE)
    grad_inputs = scatter_seq(grad_inputs.reshape(page_count, seqs, row_count, width), 1)
    grad_inputs = grad_first.reshape(page_count, row_count, width) + grad_inputs

    def place(vector, size):
        blank = jnp.zeros((width,), WIDE)
        return lax.dynamic_update_slice_in_dim(blank, vector, seq_index * size, 0)

    hidden = jnp.sum(grad_expanded, axis=0).reshape(pages, 1, ff_rows)
    hidden = lax.dynamic_update_slice_in_dim(
        jnp.zeros((pages, seqs, ff_rows), WIDE), hidden, seq_index, 1
    ).reshape(4, width)
    head_rows = jnp.stack(
        [
            place(jnp.sum(grad_query, axis=(0, 1)).reshape(span), span),
            place(jnp.sum(grad_values, axis=(0, 1)).reshape(span), span),
            jnp.sum(grad_first, axis=0),
            jnp.sum(grad_second, axis=0),
            grad_shift_one,
            grad_shift_two,
        ]
    )
    table = jnp.concatenate(
        [
            head_rows,
            hidden,
            grad_gain_one[None],
            grad_gain_two[None],
            place(grad_cell, heads_here)[None],
        ],
        axis=0,
    )
    for mask in low_seq:
        table = table + swap(table, "seq", seqs, mask)
    for mask in low_page:
        table = table + swap(table, "page", pages, mask)
    own = lax.axis_index("page") * seqs + seq_index
    mine = lax.dynamic_slice_in_dim(table, own * lanes, lanes, axis=1)
    return (
        output,
        grad_inputs,
        grad_proj,
        grad_mix,
        grad_expand,
        grad_reduce,
        mine[:10],
        mine[10:12],
        table[12, :heads],
    )


def solution(mesh):
    counts = (mesh.shape["page"], mesh.shape["seq"])
    placed = (
        P("page", "seq", None),
        P("page", "seq"),
        P("page"),
        P("page", "seq", None),
        P(("page", "seq"), None),
        P(("page", "seq"), None),
        P(("page", "seq"), None),
        P(("page", "seq"), None),
        P(None, ("page", "seq")),
        P(None, ("page", "seq")),
        P(),
    )

    def step(*args):
        return local(counts, *args)

    return jax.shard_map(
        step,
        mesh=mesh,
        in_specs=placed,
        out_specs=(
            P("page", "seq", None),
            P("page", "seq", None),
            P(("page", "seq"), None),
            P(("page", "seq"), None),
            P(("page", "seq"), None),
            P(("page", "seq"), None),
            P(None, ("page", "seq")),
            P(None, ("page", "seq")),
            P(),
        ),
        check_vma=False,
    )
```

profile of v0, /device:TPU:0, one launch (start us, length us, event | category | flops | bytes accessed | tf_op | source)
XLA Modules:
  0.0 497.4 jit_solution(14796424124524267543)
XLA Ops:
  12.6 4.2 all-to-all-start
  23.9 12.6 %all_gather.11 = s32[2,512]{1,0:T(2,128)S(1)} all-gather(s32[2,128]{1,0:T(2,128)S(1)} %copy-done.56), channel_id=1, replica_groups=mesh['page'=8,'seq'=4] {'seq'}, dimensions={1}, use_global_device_ids=true | all-gather | bytes 5120 | tf_op jit(solution)/shard_map/all_gather | solution.py:119
  42.6 13.6 %collective-permute-done.2 = bf16[128,768]{1,0:T(8,128)(2,1)S(1)} collective-permute-done((bf16[128,768]{1,0:T(8,128)(2,1)S(1)}, bf16[128,768]{1,0:T(8,128)(2,1)S(1)}, u32[]{:S(2)}, u32[]{:S(2)}) %collective-permute-start.2) | collective-permute-done | bytes 196640 | tf_op jit(solution)/shard_map/ppermute | solution.py:21
  61.4 18.7 %collective-permute-done.3 = bf16[2,128,768]{2,1,0:T(8,128)(2,1)} collective-permute-done((bf16[2,128,768]{2,1,0:T(8,128)(2,1)}, bf16[2,128,768]{2,1,0:T(8,128)(2,1)}, u32[]{:S(2)}, u32[]{:S(2)}) %collective-permute-start.3) | collective-permute-done | bytes 393248 | tf_op jit(solution)/shard_map/ppermute | solution.py:21
  89.0 7.7 %collective-permute-done.4 = bf16[2,2,128,768]{3,2,1,0:T(8,128)(2,1)S(1)} collective-permute-done((bf16[2,2,128,768]{3,2,1,0:T(8,128)(2,1)S(1)}, bf16[2,2,128,768]{3,2,1,0:T(8,128)(2,1)S(1)}, u32[]{:S(2)}, u32[]{:S(2)}) %collective-permute-start.4) | collective-permute-done | bytes 786464 | tf_op jit(solution)/shard_map/ppermute | solution.py:21
  101.9 5.0 add_convert_fusion
  106.9 5.7 %reshape.329 = bf16[2,512,3,4,64]{4,3,2,1,0:T(4,128)(2,1)} reshape(bf16[1024,768]{1,0:T(8,128)(2,1)} %add_convert_fusion) | data formatting | bytes 3145728 | tf_op jit(solution)/shard_map/reshape | solution.py:124
  112.6 4.3 fusion.69
  141.2 4.5 all-to-all-done.1
  154.6 9.5 %collective-permute-done.5 = bf16[256,1024]{1,0:T(8,128)(2,1)} collective-permute-done((bf16[256,1024]{1,0:T(8,128)(2,1)S(1)}, bf16[256,1024]{1,0:T(8,128)(2,1)}, u32[]{:S(2)}, u32[]{:S(2)}) %collective-permute-start.5) | collective-permute-done | bytes 524320 | tf_op jit(solution)/shard_map/ppermute | solution.py:21
  169.7 17.9 %collective-permute-done.9 = bf16[2,2,128,1024]{3,2,0,1:T(8,128)(2,1)} collective-permute-done((bf16[2,2,128,1024]{3,2,0,1:T(8,128)(2,1)}, bf16[2,2,128,1024]{3,2,0,1:T(8,128)(2,1)}, u32[]{:S(2)}, u32[]{:S(2)}) %collective-permute-start.9) | collective-permute-done | bytes 1048608 | tf_op jit(solution)/shard_map/ppermute | solution.py:21
  212.3 12.4 %collective-permute-done.14 = bf16[256,1024]{1,0:T(8,128)(2,1)} collective-permute-done((bf16[256,1024]{1,0:T(8,128)(2,1)}, bf16[256,1024]{1,0:T(8,128)(2,1)}, u32[]{:S(2)}, u32[]{:S(2)}) %collective-permute-start.14) | collective-permute-done | bytes 524320 | tf_op jit(solution)/shard_map/ppermute | solution.py:21
  230.1 11.5 %collective-permute-done.15 = bf16[256,1024]{1,0:T(8,128)(2,1)S(1)} collective-permute-done((bf16[256,1024]{1,0:T(8,128)(2,1)S(1)}, bf16[256,1024]{1,0:T(8,128)(2,1)S(1)}, u32[]{:S(2)}, u32[]{:S(2)}) %collective-permute-start.15) | collective-permute-done | bytes 524320 | tf_op jit(solution)/shard_map/ppermute | solution.py:21
  251.7 13.2 %copy.159 = bf16[1024,1024]{1,0:T(8,128)(2,1)} copy(bf16[1024,1024]{0,1:T(8,128)(2,1)} %bitcast.380) | data formatting | bytes 4194304 | tf_op jit(solution)/shard_map/tf,td->fd/dot_general | solution.py:164
  269.2 4.4 fusion.62
  297.0 11.9 %collective-permute-done.29 = bf16[2,2,128,1024]{3,2,1,0:T(8,128)(2,1)} collective-permute-done((bf16[2,2,128,1024]{3,2,1,0:T(8,128)(2,1)}, bf16[2,2,128,1024]{3,2,1,0:T(8,128)(2,1)}, u32[]{:S(2)}, u32[]{:S(2)}) %collective-permute-start.29) | collective-permute-done | bytes 1048608 | tf_op jit(solution)/shard_map/ppermute | solution.py:21
  311.7 19.4 %collective-permute-done.32 = bf16[2,2,128,1024]{3,2,1,0:T(8,128)(2,1)} collective-permute-done((bf16[2,2,128,1024]{3,2,1,0:T(8,128)(2,1)}, bf16[2,2,128,1024]{3,2,1,0:T(8,128)(2,1)}, u32[]{:S(2)}, u32[]{:S(2)}) %collective-permute-start.32) | collective-permute-done | bytes 1048608 | tf_op jit(solution)/shard_map/ppermute | solution.py:21
  347.5 7.2 %collective-permute-start.31 = (bf16[128,1024]{1,0:T(8,128)(2,1)S(1)}, bf16[128,1024]{1,0:T(8,128)(2,1)S(1)}, u32[]{:S(2)}, u32[]{:S(2)}) collective-permute-start(bf16[128,1024]{1,0:T(8,128)(2,1)S(1)} %fusion.52), channel_id=1, source_target_pairs={{0,16},{4,20},{8,24},{12,28},{16,0},{20,4},{24,8},{28,12},{1,17},{... | collective-permute-start | bytes 786440 | tf_op jit(solution)/shard_map/ppermute | solution.py:21
  361.1 11.2 %collective-permute-done.31 = bf16[128,1024]{1,0:T(8,128)(2,1)S(1)} collective-permute-done((bf16[128,1024]{1,0:T(8,128)(2,1)S(1)}, bf16[128,1024]{1,0:T(8,128)(2,1)S(1)}, u32[]{:S(2)}, u32[]{:S(2)}) %collective-permute-start.31) | collective-permute-done | bytes 262176 | tf_op jit(solution)/shard_map/ppermute | solution.py:21
  378.3 4.9 fusion.9
  383.2 5.4 %multiply_reduce_fusion.1 = (f32[2,4,512]{2,1,0:T(4,128)S(1)}, f32[2,4,512,512]{2,3,1,0:T(8,128)S(1)}) fusion(f32[2,4,512,512]{2,3,1,0:T(8,128)} %copy-done, f32[2,4,512]{2,1,0:T(4,128)S(1)} %bitcast.403, bf16[2,512,4,64]{1,3,2,0:T(8,128)(2,1)S(1)} %reshape.300, bf16[2,512,1,4,64]{1,4,3,0,2:T(8,128)(2,1)S(1)} %copy-done.38), kind=kOutput, calls=%fused_computation.2 | convolution fusion | flops 274722816 | bytes 17858560 | tf_op jit(solution)/shard_map/pqhe,pkhe->phqk/dot_general | solution.py:189
  416.6 5.9 %reshape.325 = bf16[2,2,2,128,768]{4,3,2,1,0:T(8,128)(2,1)} reshape(bf16[2,512,3,4,64]{4,3,2,1,0:T(4,128)(2,1)} %copy.157) | data formatting | bytes 3145728 | tf_op jit(solution)/shard_map/convert_element_type | solution.py:203
  426.3 9.7 %collective-permute-done.37 = f32[13,1024]{1,0:T(8,128)S(1)} collective-permute-done((f32[13,1024]{1,0:T(8,128)S(1)}, f32[13,1024]{1,0:T(8,128)S(1)}, u32[]{:S(2)}, u32[]{:S(2)}) %collective-permute-start.37) | collective-permute-done | bytes 53280 | tf_op jit(solution)/shard_map/ppermute | solution.py:21
  454.8 5.4 %collective-permute-done.25 = bf16[8,32,1024]{2,1,0:T(8,128)(2,1)S(1)} collective-permute-done((bf16[8,32,1024]{2,1,0:T(8,128)(2,1)S(1)}, bf16[8,32,1024]{2,1,0:T(8,128)(2,1)S(1)}, u32[]{:S(2)}, u32[]{:S(2)}) %collective-permute-start.25) | collective-permute-done | bytes 524320 | tf_op jit(solution)/shard_map/ppermute | solution.py:21
  (399 shorter events, 255.1 us)
Async XLA Ops:
  7.2 92.6 %all-gather.3.cloned.1.call-start = ((), (), s32[]{:S(2)}) async-start(), calls=%async_computation.6 | async-start | bytes 2703360 | tf_op jit(solution)/shard_map/all_gather | solution.py:98
  12.6 23.9 %all-to-all-start = ((bf16[4,32,768]{2,1,0:T(8,128)(2,1)}), bf16[4,32,768]{2,1,0:T(8,128)(2,1)S(1)}, u32[]{:S(2)}, u32[]{:S(2)}) async-start(bf16[4,32,768]{2,1,0:T(8,128)(2,1)} %reshape.285), calls=%async_computation | async-start | bytes 393216 | tf_op jit(solution)/shard_map/all_to_all | solution.py:86
  17.6 65.4 %collective-permute-start.10 = (bf16[128,1024]{1,0:T(8,128)(2,1)}, bf16[128,1024]{1,0:T(8,128)(2,1)}, u32[]{:S(2)}, u32[]{:S(2)}) collective-permute-start(bf16[128,1024]{1,0:T(8,128)(2,1)} %convert_element_type.340), channel_id=1, source_target_pairs={{0,16},{4,20},{8,24},{12,28},{16,0},{20,4},{24,8},{28,12},{1,17},{... | collective-permute-start | bytes 786440 | tf_op jit(solution)/shard_map/ppermute | solution.py:21
  20.8 39.3 %collective-permute-start = (bf16[2,128,1024]{2,1,0:T(8,128)(2,1)}, bf16[2,128,1024]{2,1,0:T(8,128)(2,1)}, u32[]{:S(2)}, u32[]{:S(2)}) collective-permute-start(bf16[2,128,1024]{2,1,0:T(8,128)(2,1)} %param.11), channel_id=1, source_target_pairs={{0,2},{1,3},{2,0},{3,1},{4,6},{5,7},{6,4},{7,5},{8,10},{9,11},{10,... | collective-permute-start | bytes 1572872 | tf_op jit(solution)/shard_map/ppermute | solution.py:21
  36.5 20.6 %all-to-all-start.2 = ((bf16[4,32,1024]{2,1,0:T(8,128)(2,1)}), bf16[4,32,1024]{2,1,0:T(8,128)(2,1)}, u32[]{:S(2)}, u32[]{:S(2)}) async-start(bf16[4,32,1024]{2,1,0:T(8,128)(2,1)} %reshape.294), calls=%async_computation.2 | async-start | bytes 524288 | tf_op jit(solution)/shard_map/all_to_all | solution.py:86
  57.1 23.0 %collective-permute-start.3 = (bf16[2,128,768]{2,1,0:T(8,128)(2,1)}, bf16[2,128,768]{2,1,0:T(8,128)(2,1)}, u32[]{:S(2)}, u32[]{:S(2)}) collective-permute-start(bf16[2,128,768]{2,1,0:T(8,128)(2,1)} %pad_maximum_fusion.15), channel_id=1, source_target_pairs={{0,8},{4,12},{8,0},{12,4},{16,24},{20,28},{24,16},{28,20},{1,9},{5... | collective-permute-start | bytes 1179656 | tf_op jit(solution)/shard_map/ppermute | solution.py:21
  57.1 27.8 %collective-permute-start.7 = (bf16[128,1024]{1,0:T(8,128)(2,1)}, bf16[128,1024]{1,0:T(8,128)(2,1)S(1)}, u32[]{:S(2)}, u32[]{:S(2)}) collective-permute-start(bf16[128,1024]{1,0:T(8,128)(2,1)} %bitcast.36), channel_id=1, source_target_pairs={{0,16},{4,20},{8,24},{12,28},{16,0},{20,4},{24,8},{28,12},{1,17},{... | collective-permute-start | bytes 786440 | tf_op jit(solution)/shard_map/ppermute | solution.py:21
  85.0 51.8 %collective-permute-start.11 = (bf16[2,128,1024]{2,1,0:T(8,128)(2,1)}, bf16[2,128,1024]{2,1,0:T(8,128)(2,1)}, u32[]{:S(2)}, u32[]{:S(2)}) collective-permute-start(bf16[2,128,1024]{2,1,0:T(8,128)(2,1)} %pad_maximum_fusion.14), channel_id=1, source_target_pairs={{0,8},{4,12},{8,0},{12,4},{16,24},{20,28},{24,16},{28,20},{1,9},{5... | collective-permute-start | bytes 1572872 | tf_op jit(solution)/shard_map/ppermute | solution.py:21
  87.0 63.9 %collective-permute-start.8 = (bf16[2,128,1024]{2,1,0:T(8,128)(2,1)}, bf16[2,128,1024]{2,1,0:T(8,128)(2,1)}, u32[]{:S(2)}, u32[]{:S(2)}) collective-permute-start(bf16[2,128,1024]{2,1,0:T(8,128)(2,1)} %pad_maximum_fusion.13), channel_id=1, source_target_pairs={{0,8},{4,12},{8,0},{12,4},{16,24},{20,28},{24,16},{28,20},{1,9},{5... | collective-permute-start | bytes 1572872 | tf_op jit(solution)/shard_map/ppermute | solution.py:21
  139.3 27.3 %collective-permute-start.12 = (bf16[2,2,128,1024]{3,2,0,1:T(8,128)(2,1)}, bf16[2,2,128,1024]{3,2,0,1:T(8,128)(2,1)}, u32[]{:S(2)}, u32[]{:S(2)}) collective-permute-start(bf16[2,2,128,1024]{3,2,0,1:T(8,128)(2,1)} %pad_maximum_fusion.10), channel_id=1, source_target_pairs={{0,4},{4,0},{8,12},{12,8},{16,20},{20,16},{24,28},{28,24},{1,5},{5... | collective-permute-start | bytes 3145736 | tf_op jit(solution)/shard_map/ppermute | solution.py:21
  153.1 34.5 %collective-permute-start.9 = (bf16[2,2,128,1024]{3,2,0,1:T(8,128)(2,1)}, bf16[2,2,128,1024]{3,2,0,1:T(8,128)(2,1)}, u32[]{:S(2)}, u32[]{:S(2)}) collective-permute-start(bf16[2,2,128,1024]{3,2,0,1:T(8,128)(2,1)} %pad_maximum_fusion.9), channel_id=1, source_target_pairs={{0,4},{4,0},{8,12},{12,8},{16,20},{20,16},{24,28},{28,24},{1,5},{5... | collective-permute-start | bytes 3145736 | tf_op jit(solution)/shard_map/ppermute | solution.py:21
  166.6 25.3 %collective-permute-start.6 = (bf16[2,256,1024]{2,1,0:T(8,128)(2,1)}, bf16[2,256,1024]{2,1,0:T(8,128)(2,1)}, u32[]{:S(2)}, u32[]{:S(2)}) collective-permute-start(bf16[2,256,1024]{2,1,0:T(8,128)(2,1)} %pad_maximum_fusion.8), channel_id=1, source_target_pairs={{0,1},{1,0},{2,3},{3,2},{4,5},{5,4},{6,7},{7,6},{8,9},{9,8},{10,11... | collective-permute-start | bytes 3145736 | tf_op jit(solution)/shard_map/ppermute | solution.py:21
  242.7 22.3 %collective-permute-start.16 = (bf16[2,256,1024]{2,1,0:T(8,128)(2,1)}, bf16[2,256,1024]{2,1,0:T(8,128)(2,1)}, u32[]{:S(2)}, u32[]{:S(2)}) collective-permute-start(bf16[2,256,1024]{2,1,0:T(8,128)(2,1)} %pad_maximum_fusion.11), channel_id=1, source_target_pairs={{0,1},{1,0},{2,3},{3,2},{4,5},{5,4},{6,7},{7,6},{8,9},{9,8},{10,11... | collective-permute-start | bytes 3145736 | tf_op jit(solution)/shard_map/ppermute | solution.py:21
  282.7 26.3 %collective-permute-start.29 = (bf16[2,2,128,1024]{3,2,1,0:T(8,128)(2,1)}, bf16[2,2,128,1024]{3,2,1,0:T(8,128)(2,1)}, u32[]{:S(2)}, u32[]{:S(2)}) collective-permute-start(bf16[2,2,128,1024]{3,2,1,0:T(8,128)(2,1)} %fusion.20), channel_id=1, source_target_pairs={{0,4},{4,0},{8,12},{12,8},{16,20},{20,16},{24,28},{28,24},{1,5},{5... | collective-permute-start | bytes 3145736 | tf_op jit(solution)/shard_map/ppermute | solution.py:21
  290.2 40.9 %collective-permute-start.32 = (bf16[2,2,128,1024]{3,2,1,0:T(8,128)(2,1)}, bf16[2,2,128,1024]{3,2,1,0:T(8,128)(2,1)}, u32[]{:S(2)}, u32[]{:S(2)}) collective-permute-start(bf16[2,2,128,1024]{3,2,1,0:T(8,128)(2,1)} %fusion.21), channel_id=1, source_target_pairs={{0,4},{4,0},{8,12},{12,8},{16,20},{20,16},{24,28},{28,24},{1,5},{5... | collective-permute-start | bytes 3145736 | tf_op jit(solution)/shard_map/ppermute | solution.py:21
  295.3 38.5 %collective-permute-start.18 = (bf16[256,1024]{1,0:T(8,128)(2,1)S(1)}, bf16[256,1024]{1,0:T(8,128)(2,1)S(1)}, u32[]{:S(2)}, u32[]{:S(2)}) collective-permute-start(bf16[256,1024]{1,0:T(8,128)(2,1)S(1)} %fusion.35), channel_id=1, source_target_pairs={{0,2},{1,3},{2,0},{3,1},{4,6},{5,7},{6,4},{7,5},{8,10},{9,11},{10,... | collective-permute-start | bytes 1572872 | tf_op jit(solution)/shard_map/ppermute | solution.py:21
  311.7 34.4 %collective-permute-start.30 = (bf16[2,128,1024]{2,1,0:T(8,128)(2,1)}, bf16[2,128,1024]{2,1,0:T(8,128)(2,1)}, u32[]{:S(2)}, u32[]{:S(2)}) collective-permute-start(bf16[2,128,1024]{2,1,0:T(8,128)(2,1)} %fusion.38), channel_id=1, source_target_pairs={{0,8},{4,12},{8,0},{12,4},{16,24},{20,28},{24,16},{28,20},{1,9},{5... | collective-permute-start | bytes 1572872 | tf_op jit(solution)/shard_map/ppermute | solution.py:21
  333.7 21.0 %collective-permute-start.33 = (bf16[2,128,1024]{2,1,0:T(8,128)(2,1)}, bf16[2,128,1024]{2,1,0:T(8,128)(2,1)}, u32[]{:S(2)}, u32[]{:S(2)}) collective-permute-start(bf16[2,128,1024]{2,1,0:T(8,128)(2,1)} %fusion.39), channel_id=1, source_target_pairs={{0,8},{4,12},{8,0},{12,4},{16,24},{20,28},{24,16},{28,20},{1,9},{5... | collective-permute-start | bytes 1572872 | tf_op jit(solution)/shard_map/ppermute | solution.py:21
  341.9 31.2 %all-to-all-start.3 = ((bf16[4,2,128,256]{3,2,1,0:T(8,128)(2,1)}), bf16[4,2,128,256]{3,2,1,0:T(8,128)(2,1)}, u32[]{:S(2)}, u32[]{:S(2)}) async-start(bf16[4,2,128,256]{3,2,1,0:T(8,128)(2,1)} %bitcast.387), calls=%async_computation.3 | async-start | bytes 1048576 | tf_op jit(solution)/shard_map/all_to_all | solution.py:86
  347.5 24.8 %collective-permute-start.31 = (bf16[128,1024]{1,0:T(8,128)(2,1)S(1)}, bf16[128,1024]{1,0:T(8,128)(2,1)S(1)}, u32[]{:S(2)}, u32[]{:S(2)}) collective-permute-start(bf16[128,1024]{1,0:T(8,128)(2,1)S(1)} %fusion.52), channel_id=1, source_target_pairs={{0,16},{4,20},{8,24},{12,28},{16,0},{20,4},{24,8},{28,12},{1,17},{... | collective-permute-start | bytes 786440 | tf_op jit(solution)/shard_map/ppermute | solution.py:21
  356.8 85.2 %collective-permute-start.34 = (bf16[128,1024]{1,0:T(8,128)(2,1)}, bf16[128,1024]{1,0:T(8,128)(2,1)}, u32[]{:S(2)}, u32[]{:S(2)}) collective-permute-start(bf16[128,1024]{1,0:T(8,128)(2,1)} %fusion.53), channel_id=1, source_target_pairs={{0,16},{4,20},{8,24},{12,28},{16,0},{20,4},{24,8},{28,12},{1,17},{... | collective-permute-start | bytes 786440 | tf_op jit(solution)/shard_map/ppermute | solution.py:21
  360.9 85.3 %collective-permute-start.24 = (bf16[8,2,32,1024]{3,2,1,0:T(8,128)(2,1)}, bf16[8,2,32,1024]{3,2,1,0:T(8,128)(2,1)}, u32[]{:S(2)}, u32[]{:S(2)}) collective-permute-start(bf16[8,2,32,1024]{3,2,1,0:T(8,128)(2,1)} %fusion.19), channel_id=1, source_target_pairs={{0,1},{1,0},{2,3},{3,2},{4,5},{5,4},{6,7},{7,6},{8,9},{9,8},{10,11... | collective-permute-start | bytes 3145736 | tf_op jit(solution)/shard_map/ppermute | solution.py:21
  373.1 70.8 %all-to-all-start.5 = ((bf16[4,32,1024]{2,1,0:T(8,128)(2,1)}), bf16[4,32,1024]{2,1,0:T(8,128)(2,1)S(1)}, u32[]{:S(2)}, u32[]{:S(2)}) async-start(bf16[4,32,1024]{2,1,0:T(8,128)(2,1)} %bitcast.123), calls=%async_computation.5 | async-start | bytes 524288 | tf_op jit(solution)/shard_map/all_to_all | solution.py:86
  414.8 35.8 %collective-permute-start.21 = (bf16[2,2,128,768]{3,2,1,0:T(8,128)(2,1)}, bf16[2,2,128,768]{3,2,1,0:T(8,128)(2,1)}, u32[]{:S(2)}, u32[]{:S(2)}) collective-permute-start(bf16[2,2,128,768]{3,2,1,0:T(8,128)(2,1)} %fusion.33), channel_id=1, source_target_pairs={{0,4},{4,0},{8,12},{12,8},{16,20},{20,16},{24,28},{28,24},{1,5},{5... | collective-permute-start | bytes 2359304 | tf_op jit(solution)/shard_map/ppermute | solution.py:21
  (85 other events, 745.2 us)
Sparse Core Ops, SparseCore 0:
  11.5 70.7 all-gather.2
where the time goes:
time: 507 us; the launch traced here: 497 us
  waiting for transfers between devices  166 us (33%)
  local copies, waits for them, and re-layouts  109 us (21%)
  starting transfers between devices  73.7 us (15%)
  other arithmetic  66.7 us (13%)
  matrix products  52.9 us (10%)
  between operations  16 us (3%)
  blocking collectives  12.6 us (2%)
    ppermute x40, waiting for transfers between devices, swap(): return lax.ppermute(values, axis, [(i, i ^ mask) for i in range(count)])  161 us
    ppermute x40, starting transfers between devices, swap(): return lax.ppermute(values, axis, [(i, i ^ mask) for i in range(count)])  50 us
    another operation x30, other arithmetic, gather_bits(): jnp.stack([jnp.where(first, values, other), jnp.where(first, other, value...  24.7 us
    unnamed x130, local copies, waits for them, and re-layouts  24.1 us
    all_to_all x6, starting transfers between devices, turn(): return lax.all_to_all(values, 'seq', 0, 0)  23.7 us
    add x15, other arithmetic, scatter_bits(): keep.astype(WIDE) + swap(send.astype(LOW), axis, count, mask).astype(WIDE)  20.7 us
    convert_element_type x3, local copies, waits for them, and re-layouts, local(): jnp.stack([grad_query, grad_keys, grad_values], axis=2).astype(LOW)  13.5 us
    dot_general x1, local copies, waits for them, and re-layouts, local(): jnp.einsum('tf,td->fd', activated_low, second_all, preferred_element_type...  13.2 us
  transfers between devices with their start and end apart: 47, of which 21 were waited for; matrix products, arithmetic and copies ran while one was open for 36% of the time, Pallas kernels for 0%

commit v1 on v0

--- a/solution.py
+++ b/solution.py
@@ -116,7 +116,24 @@
         ff_here
     )
     everything = gather_seq(tokens, 1).reshape(page_count * slots, width)
-    cells_all = lax.all_gather(cells, "seq", axis=1, tiled=True)
+    length, here, extent = (lax.axis_size("seq"), lax.axis_index("seq"), cells.shape[1])
+    upward = [(i_2, (i_2 + 1) % length) for i_2 in range(length)]
+    downward = [(i_2, (i_2 - 1) % length) for i_2 in range(length)]
+    whole = jnp.zeros((*cells.shape[:1], length * extent, *cells.shape[1 + 1 :]), cells.dtype)
+    whole = lax.dynamic_update_slice_in_dim(whole, cells, here * extent, axis=1)
+    from_left = from_right = cells
+    half = length // 2
+    for hop in range(1, half + 1):
+        from_left = lax.ppermute(from_left, "seq", upward)
+        whole = lax.dynamic_update_slice_in_dim(
+            whole, from_left, (here - hop) % length * extent, axis=1
+        )
+        if hop < length - half:
+            from_right = lax.ppermute(from_right, "seq", downward)
+            whole = lax.dynamic_update_slice_in_dim(
+                whole, from_right, (here + hop) % length * extent, axis=1
+            )
+    cells_all = whole
     bias_q = lax.dynamic_slice_in_dim(vectors[0], seq_index * span, span)
     bias_v = lax.dynamic_slice_in_dim(vectors[1], seq_index * span, span)
     bias_qkv = jnp.concatenate([bias_q, jnp.zeros_like(bias_q), bias_v])

time: 507 us -> 490 us (0.966)
  blocking collectives: 12.6 us -> 0 us
  waiting for transfers between devices: 166 us -> 177 us
  starting transfers between devices: 73.7 us -> 66.5 us
    all_gather x1 -> x0, blocking collectives: 12.6 us -> none  [local(): cells_all = lax.all_gather(cells, 'seq', axis=1, tiled=True)]
    ppermute x40, starting transfers between devices: 50 us -> 42.6 us  [swap(): return lax.ppermute(values, axis, [(i, i ^ mask) for i in range(count)])]
    ppermute x0 -> x3, waiting for transfers between devices: none -> 5.3 us  [the longest x2 5.29 us: local(): from_left = lax.ppermute(from_left, 'seq', upward)]
    unnamed x130 -> x134, local copies, waits for them, and re-layouts: 24.1 us -> 25.1 us
  transfers between devices with their start and end apart: 47 -> 50, of which waited for: 21 -> 22; matrix products, arithmetic and copies ran while one was open for 36% -> 36% of each run, Pallas kernels for 0% -> 0%
where the time goes in v1:
time: 490 us; the launch traced here: 481 us
  waiting for transfers between devices  177 us (36%)
  local copies, waits for them, and re-layouts  106 us (22%)
  starting transfers between devices  66.5 us (14%)
  other arithmetic  63.1 us (13%)
  matrix products  52.2 us (11%)
  between operations  16.2 us (3%)
    ppermute x40, waiting for transfers between devices, swap(): return lax.ppermute(values, axis, [(i, i ^ mask) for i in range(count)])  165 us
    ppermute x40, starting transfers between devices, swap(): return lax.ppermute(values, axis, [(i, i ^ mask) for i in range(count)])  42.6 us
    unnamed x134, local copies, waits for them, and re-layouts  25.1 us
    all_to_all x6, starting transfers between devices, turn(): return lax.all_to_all(values, 'seq', 0, 0)  21.4 us
    add x15, other arithmetic, scatter_bits(): keep.astype(WIDE) + swap(send.astype(LOW), axis, count, mask).astype(WIDE)  20.7 us
    another operation x30, other arithmetic, gather_bits(): jnp.stack([jnp.where(first, values, other), jnp.where(first, other, value...  20.4 us
    convert_element_type x3, local copies, waits for them, and re-layouts, local(): jnp.stack([grad_query, grad_keys, grad_values], axis=2).astype(LOW)  13.4 us
    dot_general x1, local copies, waits for them, and re-layouts, local(): jnp.einsum('tf,td->fd', activated_low, second_all, preferred_element_type...  13.2 us
  transfers between devices with their start and end apart: 50, of which 22 were waited for; matrix products, arithmetic and copies ran while one was open for 36% of the time, Pallas kernels for 0%

profile of v1, /device:TPU:0, one launch (start us, length us, event | category | flops | bytes accessed | tf_op | source)
XLA Modules:
  0.0 481.2 jit_solution(7653901714829681170)
XLA Ops:
  30.3 5.3 %collective-permute-done.7 = s32[2,128]{1,0:T(2,128)S(1)} collective-permute-done((s32[2,128]{1,0:T(2,128)S(1)}, s32[2,128]{1,0:T(2,128)S(1)}, u32[]{:S(2)}, u32[]{:S(2)}) %collective-permute-start.7) | collective-permute-done | bytes 1056 | tf_op jit(solution)/shard_map/ppermute | solution.py:127
  35.6 8.6 %collective-permute-done.2 = bf16[128,768]{1,0:T(8,128)(2,1)S(1)} collective-permute-done((bf16[128,768]{1,0:T(8,128)(2,1)S(1)}, bf16[128,768]{1,0:T(8,128)(2,1)S(1)}, u32[]{:S(2)}, u32[]{:S(2)}) %collective-permute-start.2) | collective-permute-done | bytes 196640 | tf_op jit(solution)/shard_map/ppermute | solution.py:21
  50.1 14.2 %collective-permute-done.3 = bf16[2,128,768]{2,1,0:T(8,128)(2,1)} collective-permute-done((bf16[2,128,768]{2,1,0:T(8,128)(2,1)S(1)}, bf16[2,128,768]{2,1,0:T(8,128)(2,1)}, u32[]{:S(2)}, u32[]{:S(2)}) %collective-permute-start.3) | collective-permute-done | bytes 393248 | tf_op jit(solution)/shard_map/ppermute | solution.py:21
  72.0 17.3 %collective-permute-done.4 = bf16[2,2,128,768]{3,2,1,0:T(8,128)(2,1)S(1)} collective-permute-done((bf16[2,2,128,768]{3,2,1,0:T(8,128)(2,1)S(1)}, bf16[2,2,128,768]{3,2,1,0:T(8,128)(2,1)S(1)}, u32[]{:S(2)}, u32[]{:S(2)}) %collective-permute-start.4) | collective-permute-done | bytes 786464 | tf_op jit(solution)/shard_map/ppermute | solution.py:21
  93.7 4.4 add_convert_fusion
  98.1 4.6 reshape.329
  128.4 4.9 %all-to-all-done.1 = bf16[4,2,128,256]{3,2,1,0:T(8,128)(2,1)S(1)} async-done(((bf16[4,2,128,256]{3,2,1,0:T(8,128)(2,1)}), bf16[4,2,128,256]{3,2,1,0:T(8,128)(2,1)S(1)}, u32[]{:S(2)}, u32[]{:S(2)}) %all-to-all-start.1) | async-done | bytes 524320 | tf_op jit(solution)/shard_map/all_to_all | solution.py:86
  140.6 10.2 %collective-permute-done.8 = bf16[256,1024]{1,0:T(8,128)(2,1)} collective-permute-done((bf16[256,1024]{1,0:T(8,128)(2,1)S(1)}, bf16[256,1024]{1,0:T(8,128)(2,1)}, u32[]{:S(2)}, u32[]{:S(2)}) %collective-permute-start.8) | collective-permute-done | bytes 524320 | tf_op jit(solution)/shard_map/ppermute | solution.py:21
  156.5 18.9 %collective-permute-done.12 = bf16[2,2,128,1024]{3,2,0,1:T(8,128)(2,1)} collective-permute-done((bf16[2,2,128,1024]{3,2,0,1:T(8,128)(2,1)}, bf16[2,2,128,1024]{3,2,0,1:T(8,128)(2,1)}, u32[]{:S(2)}, u32[]{:S(2)}) %collective-permute-start.12) | collective-permute-done | bytes 1048608 | tf_op jit(solution)/shard_map/ppermute | solution.py:21
  183.6 4.2 multiply_convert_fusion
  200.1 12.4 %collective-permute-done.17 = bf16[256,1024]{1,0:T(8,128)(2,1)} collective-permute-done((bf16[256,1024]{1,0:T(8,128)(2,1)}, bf16[256,1024]{1,0:T(8,128)(2,1)}, u32[]{:S(2)}, u32[]{:S(2)}) %collective-permute-start.17) | collective-permute-done | bytes 524320 | tf_op jit(solution)/shard_map/ppermute | solution.py:21
  217.9 11.5 %collective-permute-done.18 = bf16[256,1024]{1,0:T(8,128)(2,1)S(1)} collective-permute-done((bf16[256,1024]{1,0:T(8,128)(2,1)S(1)}, bf16[256,1024]{1,0:T(8,128)(2,1)S(1)}, u32[]{:S(2)}, u32[]{:S(2)}) %collective-permute-start.18) | collective-permute-done | bytes 524320 | tf_op jit(solution)/shard_map/ppermute | solution.py:21
  239.5 13.2 %copy.159 = bf16[1024,1024]{1,0:T(8,128)(2,1)} copy(bf16[1024,1024]{0,1:T(8,128)(2,1)} %bitcast.380) | data formatting | bytes 4194304 | tf_op jit(solution)/shard_map/tf,td->fd/dot_general | solution.py:181
  257.1 4.4 fusion.62
  284.2 12.5 %collective-permute-done.32 = bf16[2,2,128,1024]{3,2,1,0:T(8,128)(2,1)} collective-permute-done((bf16[2,2,128,1024]{3,2,1,0:T(8,128)(2,1)}, bf16[2,2,128,1024]{3,2,1,0:T(8,128)(2,1)}, u32[]{:S(2)}, u32[]{:S(2)}) %collective-permute-start.32) | collective-permute-done | bytes 1048608 | tf_op jit(solution)/shard_map/ppermute | solution.py:21
  299.5 19.4 %collective-permute-done.35 = bf16[2,2,128,1024]{3,2,1,0:T(8,128)(2,1)} collective-permute-done((bf16[2,2,128,1024]{3,2,1,0:T(8,128)(2,1)}, bf16[2,2,128,1024]{3,2,1,0:T(8,128)(2,1)}, u32[]{:S(2)}, u32[]{:S(2)}) %collective-permute-start.35) | collective-permute-done | bytes 1048608 | tf_op jit(solution)/shard_map/ppermute | solution.py:21
  329.7 4.1 all-to-all-start.3
  344.7 12.0 %collective-permute-done.34 = bf16[128,1024]{1,0:T(8,128)(2,1)S(1)} collective-permute-done((bf16[128,1024]{1,0:T(8,128)(2,1)S(1)}, bf16[128,1024]{1,0:T(8,128)(2,1)S(1)}, u32[]{:S(2)}, u32[]{:S(2)}) %collective-permute-start.34) | collective-permute-done | bytes 262176 | tf_op jit(solution)/shard_map/ppermute | solution.py:21
  362.6 4.9 %fusion.9 = f32[2,512,4,64]{1,3,2,0:T(8,128)S(1)} fusion(bf16[2,512,4,64]{1,3,2,0:T(8,128)(2,1)S(1)} %reshape.300, f32[2,4,512,512]{2,3,1,0:T(8,128)} %copy-done, f32[2,4,512]{2,1,0:T(4,128)S(1)} %bitcast.405), kind=kOutput, calls=%fused_computation.43 | convolution fusion | flops 272629760 | bytes 9977856 | tf_op jit(solution)/shard_map/phqk,pqhe->pkhe/dot_general | solution.py:211
  367.6 5.4 %multiply_reduce_fusion.1 = (f32[2,4,512]{2,1,0:T(4,128)S(1)}, f32[2,4,512,512]{2,3,1,0:T(8,128)S(1)}) fusion(f32[2,4,512,512]{2,3,1,0:T(8,128)} %copy-done, f32[2,4,512]{2,1,0:T(4,128)S(1)} %bitcast.406, bf16[2,512,4,64]{1,3,2,0:T(8,128)(2,1)S(1)} %reshape.300, bf16[2,512,1,4,64]{1,4,3,0,2:T(8,128)(2,1)S(1)} %copy-done.40), kind=kOutput, calls=%fused_computation.2 | convolution fusion | flops 274722816 | bytes 17858560 | tf_op jit(solution)/shard_map/pqhe,pkhe->phqk/dot_general | solution.py:206
  400.6 5.9 %reshape.325 = bf16[2,2,2,128,768]{4,3,2,1,0:T(8,128)(2,1)} reshape(bf16[2,512,3,4,64]{4,3,2,1,0:T(4,128)(2,1)} %copy.157) | data formatting | bytes 3145728 | tf_op jit(solution)/shard_map/convert_element_type | solution.py:220
  410.4 9.8 %collective-permute-done.40 = f32[13,1024]{1,0:T(8,128)S(1)} collective-permute-done((f32[13,1024]{1,0:T(8,128)S(1)}, f32[13,1024]{1,0:T(8,128)S(1)}, u32[]{:S(2)}, u32[]{:S(2)}) %collective-permute-start.40) | collective-permute-done | bytes 53280 | tf_op jit(solution)/shard_map/ppermute | solution.py:21
  420.6 4.0 collective-permute-done.41
  438.2 5.8 %collective-permute-done.28 = bf16[8,32,1024]{2,1,0:T(8,128)(2,1)S(1)} collective-permute-done((bf16[8,32,1024]{2,1,0:T(8,128)(2,1)S(1)}, bf16[8,32,1024]{2,1,0:T(8,128)(2,1)S(1)}, u32[]{:S(2)}, u32[]{:S(2)}) %collective-permute-start.28) | collective-permute-done | bytes 524320 | tf_op jit(solution)/shard_map/ppermute | solution.py:21
  (413 shorter events, 247.1 us)
Async XLA Ops:
  7.2 83.9 %all-gather.3.cloned.1.call-start = ((), (), s32[]{:S(2)}) async-start(), calls=%async_computation.6 | async-start | bytes 2703360 | tf_op jit(solution)/shard_map/all_gather | solution.py:98
  18.5 48.6 %collective-permute-start.13 = (bf16[128,1024]{1,0:T(8,128)(2,1)S(1)}, bf16[128,1024]{1,0:T(8,128)(2,1)}, u32[]{:S(2)}, u32[]{:S(2)}) collective-permute-start(bf16[128,1024]{1,0:T(8,128)(2,1)S(1)} %convert_element_type.340), channel_id=1, source_target_pairs={{0,16},{4,20},{8,24},{12,28},{16,0},{20,4},{24,8},{28,12},{1,17},{... | collective-permute-start | bytes 786440 | tf_op jit(solution)/shard_map/ppermute | solution.py:21
  21.2 28.8 %collective-permute-start = (bf16[2,128,1024]{2,1,0:T(8,128)(2,1)S(1)}, bf16[2,128,1024]{2,1,0:T(8,128)(2,1)S(1)}, u32[]{:S(2)}, u32[]{:S(2)}) collective-permute-start(bf16[2,128,1024]{2,1,0:T(8,128)(2,1)S(1)} %copy-done.56), channel_id=1, source_target_pairs={{0,2},{1,3},{2,0},{3,1},{4,6},{5,7},{6,4},{7,5},{8,10},{9,11},{10,... | collective-permute-start | bytes 1572872 | tf_op jit(solution)/shard_map/ppermute | solution.py:21
  24.6 22.0 %all-to-all-start.2 = ((bf16[4,32,1024]{2,1,0:T(8,128)(2,1)}), bf16[4,32,1024]{2,1,0:T(8,128)(2,1)S(1)}, u32[]{:S(2)}, u32[]{:S(2)}) async-start(bf16[4,32,1024]{2,1,0:T(8,128)(2,1)} %reshape.294), calls=%async_computation.2 | async-start | bytes 524288 | tf_op jit(solution)/shard_map/all_to_all | solution.py:86
  44.3 20.0 %collective-permute-start.3 = (bf16[2,128,768]{2,1,0:T(8,128)(2,1)S(1)}, bf16[2,128,768]{2,1,0:T(8,128)(2,1)}, u32[]{:S(2)}, u32[]{:S(2)}) collective-permute-start(bf16[2,128,768]{2,1,0:T(8,128)(2,1)S(1)} %pad_maximum_fusion.15), channel_id=1, source_target_pairs={{0,8},{4,12},{8,0},{12,4},{16,24},{20,28},{24,16},{28,20},{1,9},{5... | collective-permute-start | bytes 1179656 | tf_op jit(solution)/shard_map/ppermute | solution.py:21
  46.6 22.4 %collective-permute-start.10 = (bf16[128,1024]{1,0:T(8,128)(2,1)S(1)}, bf16[128,1024]{1,0:T(8,128)(2,1)S(1)}, u32[]{:S(2)}, u32[]{:S(2)}) collective-permute-start(bf16[128,1024]{1,0:T(8,128)(2,1)S(1)} %bitcast.398), channel_id=1, source_target_pairs={{0,16},{4,20},{8,24},{12,28},{16,0},{20,4},{24,8},{28,12},{1,17},{... | collective-permute-start | bytes 786440 | tf_op jit(solution)/shard_map/ppermute | solution.py:21
  65.4 23.9 %collective-permute-start.4 = (bf16[2,2,128,768]{3,2,1,0:T(8,128)(2,1)S(1)}, bf16[2,2,128,768]{3,2,1,0:T(8,128)(2,1)S(1)}, u32[]{:S(2)}, u32[]{:S(2)}) collective-permute-start(bf16[2,2,128,768]{3,2,1,0:T(8,128)(2,1)S(1)} %pad_maximum_fusion.12), channel_id=1, source_target_pairs={{0,4},{4,0},{8,12},{12,8},{16,20},{20,16},{24,28},{28,24},{1,5},{5... | collective-permute-start | bytes 2359304 | tf_op jit(solution)/shard_map/ppermute | solution.py:21
  67.0 23.7 %collective-permute-start.1 = (bf16[2,2,128,1024]{3,2,1,0:T(8,128)(2,1)S(1)}, bf16[2,2,128,1024]{3,2,1,0:T(8,128)(2,1)S(1)}, u32[]{:S(2)}, u32[]{:S(2)}) collective-permute-start(bf16[2,2,128,1024]{3,2,1,0:T(8,128)(2,1)S(1)} %pad_maximum_fusion.7), channel_id=1, source_target_pairs={{0,1},{1,0},{2,3},{3,2},{4,5},{5,4},{6,7},{7,6},{8,9},{9,8},{10,11... | collective-permute-start | bytes 3145736 | tf_op jit(solution)/shard_map/ppermute | solution.py:21
  69.0 55.5 %collective-permute-start.14 = (bf16[2,128,1024]{2,1,0:T(8,128)(2,1)}, bf16[2,128,1024]{2,1,0:T(8,128)(2,1)}, u32[]{:S(2)}, u32[]{:S(2)}) collective-permute-start(bf16[2,128,1024]{2,1,0:T(8,128)(2,1)} %pad_maximum_fusion.14), channel_id=1, source_target_pairs={{0,8},{4,12},{8,0},{12,4},{16,24},{20,28},{24,16},{28,20},{1,9},{5... | collective-permute-start | bytes 1572872 | tf_op jit(solution)/shard_map/ppermute | solution.py:21
  70.0 67.4 %collective-permute-start.11 = (bf16[2,128,1024]{2,1,0:T(8,128)(2,1)}, bf16[2,128,1024]{2,1,0:T(8,128)(2,1)}, u32[]{:S(2)}, u32[]{:S(2)}) collective-permute-start(bf16[2,128,1024]{2,1,0:T(8,128)(2,1)} %pad_maximum_fusion.13), channel_id=1, source_target_pairs={{0,8},{4,12},{8,0},{12,4},{16,24},{20,28},{24,16},{28,20},{1,9},{5... | collective-permute-start | bytes 1572872 | tf_op jit(solution)/shard_map/ppermute | solution.py:21
  127.1 26.3 %collective-permute-start.15 = (bf16[2,2,128,1024]{3,2,0,1:T(8,128)(2,1)}, bf16[2,2,128,1024]{3,2,0,1:T(8,128)(2,1)}, u32[]{:S(2)}, u32[]{:S(2)}) collective-permute-start(bf16[2,2,128,1024]{3,2,0,1:T(8,128)(2,1)} %pad_maximum_fusion.10), channel_id=1, source_target_pairs={{0,4},{4,0},{8,12},{12,8},{16,20},{20,16},{24,28},{28,24},{1,5},{5... | collective-permute-start | bytes 3145736 | tf_op jit(solution)/shard_map/ppermute | solution.py:21
  139.7 35.7 %collective-permute-start.12 = (bf16[2,2,128,1024]{3,2,0,1:T(8,128)(2,1)}, bf16[2,2,128,1024]{3,2,0,1:T(8,128)(2,1)}, u32[]{:S(2)}, u32[]{:S(2)}) collective-permute-start(bf16[2,2,128,1024]{3,2,0,1:T(8,128)(2,1)} %pad_maximum_fusion.9), channel_id=1, source_target_pairs={{0,4},{4,0},{8,12},{12,8},{16,20},{20,16},{24,28},{28,24},{1,5},{5... | collective-permute-start | bytes 3145736 | tf_op jit(solution)/shard_map/ppermute | solution.py:21
  153.2 26.4 %collective-permute-start.9 = (bf16[2,256,1024]{2,1,0:T(8,128)(2,1)}, bf16[2,256,1024]{2,1,0:T(8,128)(2,1)}, u32[]{:S(2)}, u32[]{:S(2)}) collective-permute-start(bf16[2,256,1024]{2,1,0:T(8,128)(2,1)} %pad_maximum_fusion.8), channel_id=1, source_target_pairs={{0,1},{1,0},{2,3},{3,2},{4,5},{5,4},{6,7},{7,6},{8,9},{9,8},{10,11... | collective-permute-start | bytes 3145736 | tf_op jit(solution)/shard_map/ppermute | solution.py:21
  230.5 22.3 %collective-permute-start.19 = (bf16[2,256,1024]{2,1,0:T(8,128)(2,1)}, bf16[2,256,1024]{2,1,0:T(8,128)(2,1)}, u32[]{:S(2)}, u32[]{:S(2)}) collective-permute-start(bf16[2,256,1024]{2,1,0:T(8,128)(2,1)} %pad_maximum_fusion.11), channel_id=1, source_target_pairs={{0,1},{1,0},{2,3},{3,2},{4,5},{5,4},{6,7},{7,6},{8,9},{9,8},{10,11... | collective-permute-start | bytes 3145736 | tf_op jit(solution)/shard_map/ppermute | solution.py:21
  270.5 26.3 %collective-permute-start.32 = (bf16[2,2,128,1024]{3,2,1,0:T(8,128)(2,1)}, bf16[2,2,128,1024]{3,2,1,0:T(8,128)(2,1)}, u32[]{:S(2)}, u32[]{:S(2)}) collective-permute-start(bf16[2,2,128,1024]{3,2,1,0:T(8,128)(2,1)} %fusion.20), channel_id=1, source_target_pairs={{0,4},{4,0},{8,12},{12,8},{16,20},{20,16},{24,28},{28,24},{1,5},{5... | collective-permute-start | bytes 3145736 | tf_op jit(solution)/shard_map/ppermute | solution.py:21
  278.0 40.9 %collective-permute-start.35 = (bf16[2,2,128,1024]{3,2,1,0:T(8,128)(2,1)}, bf16[2,2,128,1024]{3,2,1,0:T(8,128)(2,1)}, u32[]{:S(2)}, u32[]{:S(2)}) collective-permute-start(bf16[2,2,128,1024]{3,2,1,0:T(8,128)(2,1)} %fusion.21), channel_id=1, source_target_pairs={{0,4},{4,0},{8,12},{12,8},{16,20},{20,16},{24,28},{28,24},{1,5},{5... | collective-permute-start | bytes 3145736 | tf_op jit(solution)/shard_map/ppermute | solution.py:21
  282.5 39.0 %collective-permute-start.21 = (bf16[256,1024]{1,0:T(8,128)(2,1)S(1)}, bf16[256,1024]{1,0:T(8,128)(2,1)S(1)}, u32[]{:S(2)}, u32[]{:S(2)}) collective-permute-start(bf16[256,1024]{1,0:T(8,128)(2,1)S(1)} %fusion.35), channel_id=1, source_target_pairs={{0,2},{1,3},{2,0},{3,1},{4,6},{5,7},{6,4},{7,5},{8,10},{9,11},{10,... | collective-permute-start | bytes 1572872 | tf_op jit(solution)/shard_map/ppermute | solution.py:21
  299.5 34.4 %collective-permute-start.33 = (bf16[2,128,1024]{2,1,0:T(8,128)(2,1)}, bf16[2,128,1024]{2,1,0:T(8,128)(2,1)}, u32[]{:S(2)}, u32[]{:S(2)}) collective-permute-start(bf16[2,128,1024]{2,1,0:T(8,128)(2,1)} %fusion.38), channel_id=1, source_target_pairs={{0,8},{4,12},{8,0},{12,4},{16,24},{20,28},{24,16},{28,20},{1,9},{5... | collective-permute-start | bytes 1572872 | tf_op jit(solution)/shard_map/ppermute | solution.py:21
  329.7 27.7 %all-to-all-start.3 = ((bf16[4,2,128,256]{3,2,1,0:T(8,128)(2,1)}), bf16[4,2,128,256]{3,2,1,0:T(8,128)(2,1)}, u32[]{:S(2)}, u32[]{:S(2)}) async-start(bf16[4,2,128,256]{3,2,1,0:T(8,128)(2,1)} %bitcast.387), calls=%async_computation.3 | async-start | bytes 1048576 | tf_op jit(solution)/shard_map/all_to_all | solution.py:86
  335.3 21.4 %collective-permute-start.34 = (bf16[128,1024]{1,0:T(8,128)(2,1)S(1)}, bf16[128,1024]{1,0:T(8,128)(2,1)S(1)}, u32[]{:S(2)}, u32[]{:S(2)}) collective-permute-start(bf16[128,1024]{1,0:T(8,128)(2,1)S(1)} %fusion.52), channel_id=1, source_target_pairs={{0,16},{4,20},{8,24},{12,28},{16,0},{20,4},{24,8},{28,12},{1,17},{... | collective-permute-start | bytes 786440 | tf_op jit(solution)/shard_map/ppermute | solution.py:21
  340.3 85.2 %collective-permute-start.37 = (bf16[128,1024]{1,0:T(8,128)(2,1)}, bf16[128,1024]{1,0:T(8,128)(2,1)}, u32[]{:S(2)}, u32[]{:S(2)}) collective-permute-start(bf16[128,1024]{1,0:T(8,128)(2,1)} %fusion.53), channel_id=1, source_target_pairs={{0,16},{4,20},{8,24},{12,28},{16,0},{20,4},{24,8},{28,12},{1,17},{... | collective-permute-start | bytes 786440 | tf_op jit(solution)/shard_map/ppermute | solution.py:21
  344.5 85.5 %collective-permute-start.27 = (bf16[8,2,32,1024]{3,2,1,0:T(8,128)(2,1)}, bf16[8,2,32,1024]{3,2,1,0:T(8,128)(2,1)}, u32[]{:S(2)}, u32[]{:S(2)}) collective-permute-start(bf16[8,2,32,1024]{3,2,1,0:T(8,128)(2,1)} %fusion.19), channel_id=1, source_target_pairs={{0,1},{1,0},{2,3},{3,2},{4,5},{5,4},{6,7},{7,6},{8,9},{9,8},{10,11... | collective-permute-start | bytes 3145736 | tf_op jit(solution)/shard_map/ppermute | solution.py:21
  357.4 69.9 %all-to-all-start.5 = ((bf16[4,32,1024]{2,1,0:T(8,128)(2,1)}), bf16[4,32,1024]{2,1,0:T(8,128)(2,1)S(1)}, u32[]{:S(2)}, u32[]{:S(2)}) async-start(bf16[4,32,1024]{2,1,0:T(8,128)(2,1)} %bitcast.123), calls=%async_computation.5 | async-start | bytes 524288 | tf_op jit(solution)/shard_map/all_to_all | solution.py:86
  399.1 35.3 %collective-permute-start.24 = (bf16[2,2,128,768]{3,2,1,0:T(8,128)(2,1)}, bf16[2,2,128,768]{3,2,1,0:T(8,128)(2,1)}, u32[]{:S(2)}, u32[]{:S(2)}) collective-permute-start(bf16[2,2,128,768]{3,2,1,0:T(8,128)(2,1)} %fusion.33), channel_id=1, source_target_pairs={{0,4},{4,0},{8,12},{12,8},{16,20},{20,16},{24,28},{28,24},{1,5},{5... | collective-permute-start | bytes 2359304 | tf_op jit(solution)/shard_map/ppermute | solution.py:21
  (90 other events, 760.4 us)
Sparse Core Ops, SparseCore 0:
  11.5 74.5 all-gather.2
